TPU v7x, 32 devices: a whole 2x2x4 slice. The times are simulated.
32 devices in a mesh: rows: 8 (over y, x, core), cols: 4 (over z).
Axes of the slice: x: 2, y: 2, z: 4, core: 2. Of those that a mesh axis runs over, the one named last changes fastest.
Arguments:
- grad: bfloat16 [28672, 8192], P(('rows', 'cols')), may hold values from -8 to 8
- momentum: float32 [28672, 8192], P('rows', 'cols'), may hold values from -8 to 8
- right_basis: bfloat16 [8192, 512], P('cols'), may hold values from -0.0625 to 0.0625
Outputs:
- momentum_new: float32 [28672, 8192], P('rows', 'cols')
- left_factor: float32 [28672, 512], P('rows')
- right_new: bfloat16 [8192, 512], P('cols')
All inputs are finite; a program needn't handle non-finite values.
Results may differ from a plain program's by a relative error of at most 0.01225.
Values may be sent and summed in bfloat16 or wider, within the bound.
A program may use at most 192 MiB of HBM per device.

v0:
```python
import jax
import jax.numpy as jnp
from jax import lax
from jax.sharding import PartitionSpec as P

epsilon = 1e-06
feedback_weight = 0.05


def shift(x, s):
    n = lax.axis_size("cols")
    return lax.ppermute(x, "cols", [(i, (i + s) % n) for i in range(n)])


def flip(x, axis, stride):
    return lax.ppermute(x, axis, [(i, i ^ stride) for i in range(lax.axis_size(axis))])


def sum_everywhere(x):
    levels = lax.axis_size("rows").bit_length() - 1
    index = lax.axis_index("rows")
    for level in range(levels):
        bit = index >> level & 1
        half = x.shape[0] // 2
        keep = lax.dynamic_slice_in_dim(x, bit * half, half)
        send = lax.dynamic_slice_in_dim(x, (1 - bit) * half, half)
        x = keep + flip(send, "rows", 1 << level)
    for level in range(lax.axis_size("cols").bit_length() - 1):
        x = x + flip(x, "cols", 1 << level)
    for level in reversed(range(levels)):
        bit = index >> level & 1
        other = flip(x, "rows", 1 << level)
        low = jnp.where(bit == 0, x, other)
        high = jnp.where(bit == 0, other, x)
        x = jnp.concatenate([low, high], axis=0)
    return x


def local(grad, momentum, right_basis):
    n = lax.axis_size("cols")
    me = lax.axis_index("cols")
    deep = grad.shape[0]
    width = momentum.shape[1]
    order = sorted(range(1, n), key=lambda s: -min(s, n - s))
    tile = lambda c: lax.dynamic_slice(grad, (0, c * width), (deep, width))
    pieces = {0: tile(me)}
    for s in order:
        pieces[s] = shift(tile((me + s) % n), s)
    regrouped = jnp.zeros((n * deep, width), grad.dtype)
    blend_half = jnp.zeros((n * deep, width), jnp.bfloat16)
    panel_own = None
    for s in [0] + order:
        source = (me - s + n) % n
        chunk = lax.dynamic_slice_in_dim(momentum, source * deep, deep) + pieces[s].astype(
            jnp.float32
        )
        chunk = chunk.astype(jnp.bfloat16)
        partial = jnp.dot(chunk, right_basis, preferred_element_type=jnp.float32)
        regrouped = lax.dynamic_update_slice_in_dim(regrouped, pieces[s], source * deep, 0)
        blend_half = lax.dynamic_update_slice_in_dim(blend_half, chunk, source * deep, 0)
        if s == 0:
            panel_own = partial
        else:
            panel_own = panel_own + shift(partial.astype(jnp.bfloat16), -s).astype(jnp.float32)
    gram = sum_everywhere(jnp.dot(panel_own.T, panel_own, precision=lax.Precision.HIGHEST))
    panel = jnp.zeros((n * deep, panel_own.shape[1]), jnp.float32)
    panel = lax.dynamic_update_slice_in_dim(panel, panel_own, me * deep, 0)
    for s in range(1, n):
        panel = lax.dynamic_update_slice_in_dim(
            panel, shift(panel_own, s), (me - s + n) % n * deep, 0
        )
    lower_factor = jnp.linalg.cholesky(gram)
    left_factor = jax.scipy.linalg.solve_triangular(lower_factor, panel.T, lower=True).T
    left_half = left_factor.astype(jnp.bfloat16)
    contract_rows = (((0,), (0,)), ((), ()))
    term = lax.dot_general(blend_half, left_half, contract_rows, preferred_element_type=jnp.float32)
    projected = lax.psum(term.astype(jnp.bfloat16), "rows").astype(jnp.float32)
    column_sums = lax.psum(jnp.sum(projected * projected, axis=0), "cols")
    projected_half = projected.astype(jnp.bfloat16)
    right_new = (projected / jnp.sqrt(column_sums + epsilon)).astype(jnp.bfloat16)
    contract_cols = (((1,), (1,)), ((), ()))
    feedback = lax.dot_general(
        left_half, projected_half, contract_cols, preferred_element_type=jnp.float32
    )
    blend = momentum + regrouped.astype(jnp.float32)
    momentum_new = blend - feedback_weight * feedback
    return (momentum_new, left_factor, right_new)


def solution(mesh):
    placed = (P(("rows", "cols"), None), P("rows", "cols"), P("cols", None))
    return jax.shard_map(
        local,
        mesh=mesh,
        in_specs=placed,
        out_specs=(P("rows", "cols"), P("rows", None), P("cols", None)),
        check_vma=False,
    )
```

profile of v0, /device:TPU:0, one launch (start us, length us, event | category | flops | bytes accessed | tf_op | source)
XLA Modules:
  0.0 942.7 jit_solution(13194718705285914622)
XLA Ops:
  7.3 7.3 broadcast.196.clone
  14.6 14.9 %constant_dynamic-update-slice_fusion.3 = (bf16[3584,2048]{1,0:T(8,128)(2,1)}, bf16[896,2048]{1,0:T(8,128)(2,1)}, bf16[896,2048]{1,0:T(8,128)(2,1)}, bf16[896,2048]{1,0:T(8,128)(2,1)}, bf16[896,2048]{1,0:T(8,128)(2,1)}) fusion(bf16[3584,2048]{1,0:T(8,128)(2,1)} %broadcast.196.clone, s32[]{:T(128)S(6)} %select_n.129, bf16[896,8192]{1,0:T(8,128)(2,1)} %param.3, ...), kind=kLoop, calls=%fused_computation.90 | loop fusion | flops 5505024 | bytes 40370196 | tf_op jit(solution)/shard_map/dynamic_update_slice | solution.py:60
  35.6 79.0 %collective-permute-done.2 = bf16[896,2048]{1,0:T(8,128)(2,1)} collective-permute-done((bf16[896,2048]{1,0:T(8,128)(2,1)}, bf16[896,2048]{1,0:T(8,128)(2,1)}, u32[]{:S(2)}, u32[]{:S(2)}) %collective-permute-start.2) | collective-permute-done | bytes 3670048 | tf_op jit(solution)/shard_map/ppermute | solution.py:12
  114.6 7.2 convolution_convert_fusion.1
  121.8 176.4 %collective-permute-start.5 = (bf16[896,512]{1,0:T(8,128)(2,1)}, bf16[896,512]{1,0:T(8,128)(2,1)S(1)}, u32[]{:S(2)}, u32[]{:S(2)}) collective-permute-start(bf16[896,512]{1,0:T(8,128)(2,1)} %convolution_convert_fusion.1), channel_id=1, source_target_pairs={{0,1},{1,2},{2,3},{3,0},{4,5},{5,6},{6,7},{7,4},{8,9},{9,10},{10,1... | collective-permute-start | bytes 2752520 | tf_op jit(solution)/shard_map/ppermute | solution.py:12
  298.2 7.2 convolution_convert_fusion.2
  305.6 64.6 %collective-permute-done = bf16[896,2048]{1,0:T(8,128)(2,1)} collective-permute-done((bf16[896,2048]{1,0:T(8,128)(2,1)}, bf16[896,2048]{1,0:T(8,128)(2,1)}, u32[]{:S(2)}, u32[]{:S(2)}) %collective-permute-start) | collective-permute-done | bytes 3670048 | tf_op jit(solution)/shard_map/ppermute | solution.py:12
  370.1 7.3 convolution_convert_fusion.3
  381.5 46.5 %collective-permute-done.3 = bf16[896,512]{1,0:T(8,128)(2,1)} collective-permute-done((bf16[896,512]{1,0:T(8,128)(2,1)}, bf16[896,512]{1,0:T(8,128)(2,1)}, u32[]{:S(2)}, u32[]{:S(2)}) %collective-permute-start.3) | collective-permute-done | bytes 917536 | tf_op jit(solution)/shard_map/ppermute | solution.py:12
  445.4 6.9 collective-permute-done.7
  469.4 7.1 broadcast.196.clone.1
  482.4 10.4 %constant_dynamic-update-slice_fusion.2 = (bf16[3584,2048]{1,0:T(8,128)(2,1)}, bf16[3584,2048]{1,0:T(8,128)(2,1)}) fusion(bf16[3584,2048]{1,0:T(8,128)(2,1)} %get-tuple-element.24, s32[]{:T(128)S(6)} %select_n.132, bf16[896,2048]{1,0:T(8,128)(2,1)} %collective-permute-done, f32[3584,2048]{1,0:T(8,128)} %param.4, ...), kind=kLoop, calls=%fused_computation.89 | loop fusion | flops 5505024 | bytes 18350084 | tf_op jit(solution)/shard_map/dynamic_update_slice | solution.py:60
  499.3 10.4 %constant_dynamic-update-slice_fusion.1 = (bf16[3584,2048]{1,0:T(8,128)(2,1)}, bf16[3584,2048]{1,0:T(8,128)(2,1)}) fusion(bf16[3584,2048]{1,0:T(8,128)(2,1)} %get-tuple-element.35, s32[]{:T(128)S(6)} %select_n.136, bf16[896,2048]{1,0:T(8,128)(2,1)} %collective-permute-done.1, f32[3584,2048]{1,0:T(8,128)} %param.4, bf16[3584,2048]{1,0:T(8,128)(2,1)} %get-tuple-element.36), kind=kLoop, calls=%fused_computation.88 | loop fusion | flops 5505024 | bytes 18350084 | tf_op jit(solution)/shard_map/dynamic_update_slice | solution.py:60
  509.9 10.4 %constant_dynamic-update-slice_fusion = (bf16[3584,2048]{1,0:T(8,128)(2,1)}, bf16[3584,2048]{1,0:T(8,128)(2,1)}) fusion(bf16[3584,2048]{1,0:T(8,128)(2,1)} %get-tuple-element.33, s32[]{:T(128)S(6)} %select_n.138, bf16[896,2048]{1,0:T(8,128)(2,1)} %collective-permute-done.2, f32[3584,2048]{1,0:T(8,128)} %param.4, bf16[3584,2048]{1,0:T(8,128)(2,1)} %get-tuple-element.34), kind=kLoop, calls=%fused_computation.87 | loop fusion | flops 5505024 | bytes 18350084 | tf_op jit(solution)/shard_map/dynamic_update_slice | solution.py:60
  520.3 17.4 %collective-permute-done.14 = f32[896,512]{1,0:T(8,128)S(1)} collective-permute-done((f32[896,512]{1,0:T(8,128)S(1)}, f32[896,512]{1,0:T(8,128)S(1)}, u32[]{:S(2)}, u32[]{:S(2)}) %collective-permute-start.14) | collective-permute-done | bytes 1835040 | tf_op jit(solution)/shard_map/ppermute | solution.py:12
  539.0 75.1 %collective-permute-done.15 = f32[896,512]{1,0:T(8,128)S(1)} collective-permute-done((f32[896,512]{1,0:T(8,128)S(1)}, f32[896,512]{1,0:T(8,128)S(1)}, u32[]{:S(2)}, u32[]{:S(2)}) %collective-permute-start.15) | collective-permute-done | bytes 1835040 | tf_op jit(solution)/shard_map/ppermute | solution.py:12
  617.6 11.7 %cholesky.104 = f32[128,128]{1,0:T(8,128)S(1)} custom-call(f32[128,128]{1,0:T(8,128)S(1)} %cholesky.266), custom_call_target="Cholesky" | custom-call | tf_op jit(solution)/shard_map/jit(cholesky)/cholesky | solution.py:72
  629.5 9.8 %custom-call.31 = f32[1,128,128]{1,2,0:T(8,128)S(1)} custom-call(f32[1,128,128]{2,1,0:T(8,128)S(1)} %get-tuple-element.52), custom_call_target="InvertDiagBlocksLowerTriangular" | custom-call | tf_op jit(solution)/shard_map/jit(cholesky)/cholesky | solution.py:72
  640.0 12.2 %cholesky.217 = f32[128,128]{1,0:T(8,128)S(1)} custom-call(f32[128,128]{1,0:T(8,128)S(1)} %cholesky.270), custom_call_target="Cholesky" | custom-call | tf_op jit(solution)/shard_map/jit(cholesky)/cholesky | solution.py:72
  652.2 9.8 %custom-call.32 = f32[1,128,128]{1,2,0:T(8,128)S(1)} custom-call(f32[1,128,128]{2,1,0:T(8,128)S(1)} %get-tuple-element.49), custom_call_target="InvertDiagBlocksLowerTriangular" | custom-call | tf_op jit(solution)/shard_map/jit(cholesky)/cholesky | solution.py:72
  662.7 11.7 %cholesky.238 = f32[128,128]{1,0:T(8,128)S(1)} custom-call(f32[128,128]{1,0:T(8,128)S(1)} %cholesky.275), custom_call_target="Cholesky" | custom-call | tf_op jit(solution)/shard_map/jit(cholesky)/cholesky | solution.py:72
  674.4 9.8 %custom-call.33 = f32[1,128,128]{1,2,0:T(8,128)S(1)} custom-call(f32[1,128,128]{2,1,0:T(8,128)S(1)} %get-tuple-element.46), custom_call_target="InvertDiagBlocksLowerTriangular" | custom-call | tf_op jit(solution)/shard_map/jit(cholesky)/cholesky | solution.py:72
  684.8 11.9 %cholesky.255 = f32[128,128]{1,0:T(8,128)S(1)} custom-call(f32[128,128]{1,0:T(8,128)S(1)} %convolution_subtract_fusion.2), custom_call_target="Cholesky" | custom-call | tf_op jit(solution)/shard_map/jit(cholesky)/cholesky | solution.py:72
  701.5 7.7 while.1
  709.2 39.3 %custom-call.34 = f32[4,128,128]{1,2,0:T(8,128)S(1)} custom-call(f32[4,128,128]{2,1,0:T(8,128)S(1)} %get-tuple-element.10), custom_call_target="InvertDiagBlocksLowerTriangular" | custom-call | tf_op jit(solution)/shard_map/jit(_solve_triangular)/triangular_solve | solution.py:73
  758.1 6.6 fusion.8
  768.1 9.2 fusion
  782.0 12.3 %convolution_convert_fusion = bf16[2048,512]{1,0:T(8,128)(2,1)} fusion(bf16[3584,2048]{1,0:T(8,128)(2,1)} %get-tuple-element.31, f32[128,3584]{1,0:T(8,128)S(1)} %fusion.12, f32[128,3584]{1,0:T(8,128)S(1)} %fusion.13, f32[128,3584]{1,0:T(8,128)S(1)} %fusion.14, f32[128,3584]{1,0:T(8,128)S(1)} %fusion.15), kind=kOutput, calls=%fused_computation.23 | convolution fusion | flops 7531921408 | bytes 24117248 | tf_op jit(solution)/shard_map/dot_general | solution.py:76
  799.4 8.4 copy.9
  807.8 82.9 %all-reduce.3.cloned.1.call-done = bf16[2048,512]{1,0:T(8,128)(2,1)} async-done(((bf16[2048,512]{1,0:T(8,128)(2,1)}), bf16[2048,512]{1,0:T(8,128)(2,1)}) %all-reduce.3.cloned.1.call-update) | async-done | bytes 2097168 | tf_op jit(solution)/shard_map/psum | solution.py:77
  892.7 11.7 %psum.15 = f32[512]{0:T(512)S(1)} all-reduce(f32[512]{0:T(512)S(1)} %fusion.6), channel_id=1, replica_groups=mesh['rows'=8,'cols'=4] {'cols'}, use_global_device_ids=true, to_apply=%region_10.11 | all-reduce | flops 512 | bytes 4096 | tf_op jit(solution)/shard_map/psum | solution.py:78
  904.5 27.9 %multiply_subtract_fusion = f32[3584,2048]{1,0:T(8,128)} fusion(f32[3584,2048]{1,0:T(8,128)} %param.4, bf16[3584,2048]{1,0:T(8,128)(2,1)} %get-tuple-element.32, bf16[2048,512]{1,0:T(8,128)(2,1)} %all-reduce.3.cloned.1.call-done, f32[128,3584]{1,0:T(8,128)} %copy-done.5, f32[128,3584]{1,0:T(8,128)} %copy-done.4, f32[128,3584]{1,0:T(8,128)} %copy-done.3, ...), kind=kOutput, calls=%fused_computation.2 | convolution fusion | flops 7560232960 | bytes 82837504 | tf_op jit(solution)/shard_map/dot_general | solution.py:82
  (109 shorter events, 102.4 us)
Async XLA Ops:
  7.2 107.4 %copy-start = (bf16[2048,512]{1,0:T(8,128)(2,1)S(1)}, bf16[2048,512]{1,0:T(8,128)(2,1)}, u32[]{:S(2)}) copy-start(bf16[2048,512]{1,0:T(8,128)(2,1)} %param.5) | copy-start | bytes 6291460
  7.2 883.5 %all-reduce.3.cloned.1.call-start = ((), (), s32[]{:S(2)}) async-start(), calls=%async_computation | async-start | bytes 4194304 | tf_op jit(solution)/shard_map/psum | solution.py:77
  29.5 85.1 %collective-permute-start.2 = (bf16[896,2048]{1,0:T(8,128)(2,1)}, bf16[896,2048]{1,0:T(8,128)(2,1)}, u32[]{:S(2)}, u32[]{:S(2)}) collective-permute-start(bf16[896,2048]{1,0:T(8,128)(2,1)} %get-tuple-element.29), channel_id=1, source_target_pairs={{0,3},{1,0},{2,1},{3,2},{4,7},{5,4},{6,5},{7,6},{8,11},{9,8},{10,9... | collective-permute-start | bytes 11010056 | tf_op jit(solution)/shard_map/ppermute | solution.py:12
  34.5 263.6 %collective-permute-start.1 = (bf16[896,2048]{1,0:T(8,128)(2,1)}, bf16[896,2048]{1,0:T(8,128)(2,1)}, u32[]{:S(2)}, u32[]{:S(2)}) collective-permute-start(bf16[896,2048]{1,0:T(8,128)(2,1)} %get-tuple-element.30), channel_id=1, source_target_pairs={{0,1},{1,2},{2,3},{3,0},{4,5},{5,6},{6,7},{7,4},{8,9},{9,10},{10,1... | collective-permute-start | bytes 11010056 | tf_op jit(solution)/shard_map/ppermute | solution.py:12
  34.5 335.6 %collective-permute-start = (bf16[896,2048]{1,0:T(8,128)(2,1)}, bf16[896,2048]{1,0:T(8,128)(2,1)}, u32[]{:S(2)}, u32[]{:S(2)}) collective-permute-start(bf16[896,2048]{1,0:T(8,128)(2,1)} %get-tuple-element.28), channel_id=1, source_target_pairs={{0,2},{1,3},{2,0},{3,1},{4,6},{5,7},{6,4},{7,5},{8,10},{9,11},{10,... | collective-permute-start | bytes 11010056 | tf_op jit(solution)/shard_map/ppermute | solution.py:12
  121.8 259.7 %collective-permute-start.5 = (bf16[896,512]{1,0:T(8,128)(2,1)}, bf16[896,512]{1,0:T(8,128)(2,1)S(1)}, u32[]{:S(2)}, u32[]{:S(2)}) collective-permute-start(bf16[896,512]{1,0:T(8,128)(2,1)} %convolution_convert_fusion.1), channel_id=1, source_target_pairs={{0,1},{1,2},{2,3},{3,0},{4,5},{5,6},{6,7},{7,4},{8,9},{9,10},{10,1... | collective-permute-start | bytes 2752520 | tf_op jit(solution)/shard_map/ppermute | solution.py:12
  305.4 76.1 %collective-permute-start.4 = (bf16[896,512]{1,0:T(8,128)(2,1)}, bf16[896,512]{1,0:T(8,128)(2,1)}, u32[]{:S(2)}, u32[]{:S(2)}) collective-permute-start(bf16[896,512]{1,0:T(8,128)(2,1)} %convolution_convert_fusion.2), channel_id=1, source_target_pairs={{0,3},{1,0},{2,1},{3,2},{4,7},{5,4},{6,5},{7,6},{8,11},{9,8},{10,9... | collective-permute-start | bytes 2752520 | tf_op jit(solution)/shard_map/ppermute | solution.py:12
  377.4 50.6 %collective-permute-start.3 = (bf16[896,512]{1,0:T(8,128)(2,1)}, bf16[896,512]{1,0:T(8,128)(2,1)}, u32[]{:S(2)}, u32[]{:S(2)}) collective-permute-start(bf16[896,512]{1,0:T(8,128)(2,1)} %convolution_convert_fusion.3), channel_id=1, source_target_pairs={{0,2},{1,3},{2,0},{3,1},{4,6},{5,7},{6,4},{7,5},{8,10},{9,11},{10,... | collective-permute-start | bytes 2752520 | tf_op jit(solution)/shard_map/ppermute | solution.py:12
  439.7 2.3 collective-permute-start.6
  443.0 0.8 copy-start.6
  443.9 8.4 collective-permute-start.7
  453.4 7.6 collective-permute-start.8
  461.2 6.7 collective-permute-start.9
  467.9 12.9 %collective-permute-start.10 = (f32[64,512]{0,1:T(8,128)S(1)}, f32[64,512]{0,1:T(8,128)S(1)}, u32[]{:S(2)}, u32[]{:S(2)}) collective-permute-start(f32[64,512]{0,1:T(8,128)S(1)} %add.225), channel_id=1, source_target_pairs={{0,2},{1,3},{2,0},{3,1},{4,6},{5,7},{6,4},{7,5},{8,10},{9,11},{10,... | collective-permute-start | bytes 393224 | tf_op jit(solution)/shard_map/ppermute | solution.py:16
  480.8 16.7 %collective-permute-start.11 = (f32[64,512]{0,1:T(8,128)S(1)}, f32[64,512]{0,1:T(8,128)S(1)}, u32[]{:S(2)}, u32[]{:S(2)}) collective-permute-start(f32[64,512]{0,1:T(8,128)S(1)} %add.226), channel_id=1, source_target_pairs={{0,16},{4,20},{8,24},{12,28},{16,0},{20,4},{24,8},{28,12},{1,17},{... | collective-permute-start | bytes 393224 | tf_op jit(solution)/shard_map/ppermute | solution.py:16
  492.8 44.8 %collective-permute-start.14 = (f32[896,512]{1,0:T(8,128)S(1)}, f32[896,512]{1,0:T(8,128)S(1)}, u32[]{:S(2)}, u32[]{:S(2)}) collective-permute-start(f32[896,512]{1,0:T(8,128)S(1)} %get-tuple-element.23), channel_id=1, source_target_pairs={{0,1},{1,2},{2,3},{3,0},{4,5},{5,6},{6,7},{7,4},{8,9},{9,10},{10,1... | collective-permute-start | bytes 5505032 | tf_op jit(solution)/shard_map/ppermute | solution.py:12
  494.5 119.6 %collective-permute-start.15 = (f32[896,512]{1,0:T(8,128)S(1)}, f32[896,512]{1,0:T(8,128)S(1)}, u32[]{:S(2)}, u32[]{:S(2)}) collective-permute-start(f32[896,512]{1,0:T(8,128)S(1)} %get-tuple-element.23), channel_id=1, source_target_pairs={{0,2},{1,3},{2,0},{3,1},{4,6},{5,7},{6,4},{7,5},{8,10},{9,11},{10,... | collective-permute-start | bytes 5505032 | tf_op jit(solution)/shard_map/ppermute | solution.py:12
  495.3 120.2 %collective-permute-start.16 = (f32[896,512]{1,0:T(8,128)S(1)}, f32[896,512]{1,0:T(8,128)S(1)}, u32[]{:S(2)}, u32[]{:S(2)}) collective-permute-start(f32[896,512]{1,0:T(8,128)S(1)} %get-tuple-element.23), channel_id=1, source_target_pairs={{0,3},{1,0},{2,1},{3,2},{4,7},{5,4},{6,5},{7,6},{8,11},{9,8},{10,9... | collective-permute-start | bytes 5505032 | tf_op jit(solution)/shard_map/ppermute | solution.py:12
  497.7 11.9 %collective-permute-start.12 = (f32[128,512]{0,1:T(8,128)S(1)}, f32[128,512]{0,1:T(8,128)S(1)}, u32[]{:S(2)}, u32[]{:S(2)}) collective-permute-start(f32[128,512]{0,1:T(8,128)S(1)} %pad_maximum_fusion.2), channel_id=1, source_target_pairs={{0,8},{4,12},{8,0},{12,4},{16,24},{20,28},{24,16},{28,20},{1,9},{5... | collective-permute-start | bytes 786440 | tf_op jit(solution)/shard_map/ppermute | solution.py:16
  509.8 107.0 %collective-permute-start.13 = (f32[256,512]{0,1:T(8,128)S(1)}, f32[256,512]{0,1:T(8,128)S(1)}, u32[]{:S(2)}, u32[]{:S(2)}) collective-permute-start(f32[256,512]{0,1:T(8,128)S(1)} %pad_maximum_fusion.1), channel_id=1, source_target_pairs={{0,4},{4,0},{8,12},{12,8},{16,20},{20,16},{24,28},{28,24},{1,5},{5... | collective-permute-start | bytes 1572872 | tf_op jit(solution)/shard_map/ppermute | solution.py:16
  751.7 42.6 %copy-start.2 = (f32[128,3584]{1,0:T(8,128)}, f32[128,3584]{1,0:T(8,128)S(1)}, u32[]{:S(2)}) copy-start(f32[128,3584]{1,0:T(8,128)S(1)} %fusion.15) | copy-start | bytes 5505028
  758.1 22.6 %copy-start.3 = (f32[128,3584]{1,0:T(8,128)}, f32[128,3584]{1,0:T(8,128)S(1)}, u32[]{:S(2)}) copy-start(f32[128,3584]{1,0:T(8,128)S(1)} %fusion.14) | copy-start | bytes 5505028
  768.1 12.7 %copy-start.4 = (f32[128,3584]{1,0:T(8,128)}, f32[128,3584]{1,0:T(8,128)S(1)}, u32[]{:S(2)}) copy-start(f32[128,3584]{1,0:T(8,128)S(1)} %fusion.13) | copy-start | bytes 5505028
  780.8 1.3 copy-start.5
  904.5 31.2 %copy-start.1 = (bf16[2048,512]{1,0:T(8,128)(2,1)S(1)}, bf16[2048,512]{1,0:T(8,128)(2,1)}, u32[]{:S(2)}) copy-start(bf16[2048,512]{1,0:T(8,128)(2,1)} %param.5) | copy-start | bytes 6291460
Sparse Core Ops, SparseCore 0:
  794.4 96.1 all-reduce.2
where the time goes:
time: 948 us; the launch traced here: 943 us
  waiting for transfers between devices  387 us (41%)
  starting transfers between devices  195 us (21%)
  other arithmetic  181 us (19%)
  matrix products  103 us (11%)
  local copies, waits for them, and re-layouts  46.3 us (5%)
  between operations  17.2 us (2%)
  blocking collectives  11.7 us (1%)
    ppermute x9, waiting for transfers between devices, shift(): return lax.ppermute(x, 'cols', [(i, (i + s) % n) for i in range(n)])  283 us
    ppermute x9, starting transfers between devices, shift(): return lax.ppermute(x, 'cols', [(i, (i + s) % n) for i in range(n)])  187 us
    psum x1, waiting for transfers between devices, local(): projected = lax.psum(term.astype(jnp.bfloat16), 'rows').astype(jnp.float32)  82.9 us
    another operation x14, other arithmetic, local(): lower_factor = jnp.linalg.cholesky(gram)  79.1 us
    dynamic_update_slice x4, other arithmetic, local(): lax.dynamic_update_slice_in_dim(blend_half, chunk, source * deep, 0)  46 us
    another operation x3, other arithmetic, local(): jax.scipy.linalg.solve_triangular(lower_factor, panel.T, lower=True)  39.4 us
    another operation x7, matrix products, local(): jax.scipy.linalg.solve_triangular(lower_factor, panel.T, lower=True)  32.2 us
    dot_general x1, matrix products, local(): lax.dot_general(left_half, projected_half, contract_cols, preferred_eleme...  27.9 us
  transfers between devices with their start and end apart: 18, of which 10 were waited for; matrix products, arithmetic and copies ran while one was open for 9% of the time, Pallas kernels for 0%

commit v1 on v0

--- a/solution.py
+++ b/solution.py
@@ -74,7 +74,9 @@
     left_half = left_factor.astype(jnp.bfloat16)
     contract_rows = (((0,), (0,)), ((), ()))
     term = lax.dot_general(blend_half, left_half, contract_rows, preferred_element_type=jnp.float32)
-    projected = lax.psum(term.astype(jnp.bfloat16), "rows").astype(jnp.float32)
+    projected = jnp.sum(lax.all_gather(term.astype(jnp.bfloat16), "rows"), axis=0).astype(
+        jnp.float32
+    )
     column_sums = lax.psum(jnp.sum(projected * projected, axis=0), "cols")
     projected_half = projected.astype(jnp.bfloat16)
     right_new = (projected / jnp.sqrt(column_sums + epsilon)).astype(jnp.bfloat16)

time: 948 us -> 986 us (1.040)
  waiting for transfers between devices: 387 us -> 416 us
    all_gather x0 -> x1, waiting for transfers between devices: none -> 111 us  [local(): lax.all_gather(term.astype(jnp.bfloat16), 'rows')]
    psum x1 -> x0, waiting for transfers between devices: 82.9 us -> none  [local(): projected = lax.psum(term.astype(jnp.bfloat16), 'rows').astype(jnp.float32)]
where the time goes in v1:
time: 986 us; the launch traced here: 980 us
  waiting for transfers between devices  416 us (42%)
  starting transfers between devices  195 us (20%)
  other arithmetic  189 us (19%)
  matrix products  103 us (10%)
  local copies, waits for them, and re-layouts  48.1 us (5%)
  between operations  17.2 us (2%)
  blocking collectives  11.7 us (1%)
    ppermute x9, waiting for transfers between devices, shift(): return lax.ppermute(x, 'cols', [(i, (i + s) % n) for i in range(n)])  283 us
    ppermute x9, starting transfers between devices, shift(): return lax.ppermute(x, 'cols', [(i, (i + s) % n) for i in range(n)])  187 us
    all_gather x1, waiting for transfers between devices, local(): lax.all_gather(term.astype(jnp.bfloat16), 'rows')  111 us
    another operation x14, other arithmetic, local(): lower_factor = jnp.linalg.cholesky(gram)  79 us
    dynamic_update_slice x4, other arithmetic, local(): lax.dynamic_update_slice_in_dim(blend_half, chunk, source * deep, 0)  46 us
    another operation x3, other arithmetic, local(): jax.scipy.linalg.solve_triangular(lower_factor, panel.T, lower=True)  39.4 us
    another operation x7, matrix products, local(): jax.scipy.linalg.solve_triangular(lower_factor, panel.T, lower=True)  32.2 us
    dot_general x1, matrix products, local(): lax.dot_general(left_half, projected_half, contract_cols, preferred_eleme...  27.9 us
  transfers between devices with their start and end apart: 18, of which 10 were waited for; matrix products, arithmetic and copies ran while one was open for 9% of the time, Pallas kernels for 0%

profile of v1, /device:TPU:0, one launch (start us, length us, event | category | flops | bytes accessed | tf_op | source)
XLA Modules:
  0.0 980.4 jit_solution(10437939613213214624)
XLA Ops:
  7.3 7.3 broadcast.196.clone
  14.6 14.9 %constant_dynamic-update-slice_fusion.3 = (bf16[3584,2048]{1,0:T(8,128)(2,1)}, bf16[896,2048]{1,0:T(8,128)(2,1)}, bf16[896,2048]{1,0:T(8,128)(2,1)}, bf16[896,2048]{1,0:T(8,128)(2,1)}, bf16[896,2048]{1,0:T(8,128)(2,1)}) fusion(bf16[3584,2048]{1,0:T(8,128)(2,1)} %broadcast.196.clone, s32[]{:T(128)S(6)} %select_n.129, bf16[896,8192]{1,0:T(8,128)(2,1)} %param.3, ...), kind=kLoop, calls=%fused_computation.90 | loop fusion | flops 5505024 | bytes 40370196 | tf_op jit(solution)/shard_map/dynamic_update_slice | solution.py:60
  35.6 79.0 %collective-permute-done.2 = bf16[896,2048]{1,0:T(8,128)(2,1)} collective-permute-done((bf16[896,2048]{1,0:T(8,128)(2,1)}, bf16[896,2048]{1,0:T(8,128)(2,1)}, u32[]{:S(2)}, u32[]{:S(2)}) %collective-permute-start.2) | collective-permute-done | bytes 3670048 | tf_op jit(solution)/shard_map/ppermute | solution.py:12
  114.6 7.2 convolution_convert_fusion.1
  121.8 176.3 %collective-permute-start.5 = (bf16[896,512]{1,0:T(8,128)(2,1)}, bf16[896,512]{1,0:T(8,128)(2,1)S(1)}, u32[]{:S(2)}, u32[]{:S(2)}) collective-permute-start(bf16[896,512]{1,0:T(8,128)(2,1)} %convolution_convert_fusion.1), channel_id=1, source_target_pairs={{0,1},{1,2},{2,3},{3,0},{4,5},{5,6},{6,7},{7,4},{8,9},{9,10},{10,1... | collective-permute-start | bytes 2752520 | tf_op jit(solution)/shard_map/ppermute | solution.py:12
  298.2 7.2 convolution_convert_fusion.2
  305.6 64.6 %collective-permute-done = bf16[896,2048]{1,0:T(8,128)(2,1)} collective-permute-done((bf16[896,2048]{1,0:T(8,128)(2,1)}, bf16[896,2048]{1,0:T(8,128)(2,1)}, u32[]{:S(2)}, u32[]{:S(2)}) %collective-permute-start) | collective-permute-done | bytes 3670048 | tf_op jit(solution)/shard_map/ppermute | solution.py:12
  370.2 7.2 convolution_convert_fusion.3
  381.5 46.5 %collective-permute-done.3 = bf16[896,512]{1,0:T(8,128)(2,1)} collective-permute-done((bf16[896,512]{1,0:T(8,128)(2,1)}, bf16[896,512]{1,0:T(8,128)(2,1)}, u32[]{:S(2)}, u32[]{:S(2)}) %collective-permute-start.3) | collective-permute-done | bytes 917536 | tf_op jit(solution)/shard_map/ppermute | solution.py:12
  445.4 6.9 collective-permute-done.7
  469.4 7.1 broadcast.196.clone.1
  482.4 10.4 %constant_dynamic-update-slice_fusion.2 = (bf16[3584,2048]{1,0:T(8,128)(2,1)}, bf16[3584,2048]{1,0:T(8,128)(2,1)}) fusion(bf16[3584,2048]{1,0:T(8,128)(2,1)} %get-tuple-element.24, s32[]{:T(128)S(6)} %select_n.132, bf16[896,2048]{1,0:T(8,128)(2,1)} %collective-permute-done, f32[3584,2048]{1,0:T(8,128)} %param.4, ...), kind=kLoop, calls=%fused_computation.89 | loop fusion | flops 5505024 | bytes 18350084 | tf_op jit(solution)/shard_map/dynamic_update_slice | solution.py:60
  499.3 10.4 %constant_dynamic-update-slice_fusion.1 = (bf16[3584,2048]{1,0:T(8,128)(2,1)}, bf16[3584,2048]{1,0:T(8,128)(2,1)}) fusion(bf16[3584,2048]{1,0:T(8,128)(2,1)} %get-tuple-element.35, s32[]{:T(128)S(6)} %select_n.136, bf16[896,2048]{1,0:T(8,128)(2,1)} %collective-permute-done.1, f32[3584,2048]{1,0:T(8,128)} %param.4, bf16[3584,2048]{1,0:T(8,128)(2,1)} %get-tuple-element.36), kind=kLoop, calls=%fused_computation.88 | loop fusion | flops 5505024 | bytes 18350084 | tf_op jit(solution)/shard_map/dynamic_update_slice | solution.py:60
  509.9 10.4 %constant_dynamic-update-slice_fusion = (bf16[3584,2048]{1,0:T(8,128)(2,1)}, bf16[3584,2048]{1,0:T(8,128)(2,1)}) fusion(bf16[3584,2048]{1,0:T(8,128)(2,1)} %get-tuple-element.33, s32[]{:T(128)S(6)} %select_n.138, bf16[896,2048]{1,0:T(8,128)(2,1)} %collective-permute-done.2, f32[3584,2048]{1,0:T(8,128)} %param.4, bf16[3584,2048]{1,0:T(8,128)(2,1)} %get-tuple-element.34), kind=kLoop, calls=%fused_computation.87 | loop fusion | flops 5505024 | bytes 18350084 | tf_op jit(solution)/shard_map/dynamic_update_slice | solution.py:60
  520.3 17.4 %collective-permute-done.14 = f32[896,512]{1,0:T(8,128)S(1)} collective-permute-done((f32[896,512]{1,0:T(8,128)S(1)}, f32[896,512]{1,0:T(8,128)S(1)}, u32[]{:S(2)}, u32[]{:S(2)}) %collective-permute-start.14) | collective-permute-done | bytes 1835040 | tf_op jit(solution)/shard_map/ppermute | solution.py:12
  539.0 75.1 %collective-permute-done.15 = f32[896,512]{1,0:T(8,128)S(1)} collective-permute-done((f32[896,512]{1,0:T(8,128)S(1)}, f32[896,512]{1,0:T(8,128)S(1)}, u32[]{:S(2)}, u32[]{:S(2)}) %collective-permute-start.15) | collective-permute-done | bytes 1835040 | tf_op jit(solution)/shard_map/ppermute | solution.py:12
  617.6 11.7 %cholesky.104 = f32[128,128]{1,0:T(8,128)S(1)} custom-call(f32[128,128]{1,0:T(8,128)S(1)} %cholesky.266), custom_call_target="Cholesky" | custom-call | tf_op jit(solution)/shard_map/jit(cholesky)/cholesky | solution.py:72
  629.5 9.8 %custom-call.31 = f32[1,128,128]{1,2,0:T(8,128)S(1)} custom-call(f32[1,128,128]{2,1,0:T(8,128)S(1)} %get-tuple-element.52), custom_call_target="InvertDiagBlocksLowerTriangular" | custom-call | tf_op jit(solution)/shard_map/jit(cholesky)/cholesky | solution.py:72
  640.0 12.2 %cholesky.217 = f32[128,128]{1,0:T(8,128)S(1)} custom-call(f32[128,128]{1,0:T(8,128)S(1)} %cholesky.270), custom_call_target="Cholesky" | custom-call | tf_op jit(solution)/shard_map/jit(cholesky)/cholesky | solution.py:72
  652.2 9.8 %custom-call.32 = f32[1,128,128]{1,2,0:T(8,128)S(1)} custom-call(f32[1,128,128]{2,1,0:T(8,128)S(1)} %get-tuple-element.49), custom_call_target="InvertDiagBlocksLowerTriangular" | custom-call | tf_op jit(solution)/shard_map/jit(cholesky)/cholesky | solution.py:72
  662.7 11.7 %cholesky.238 = f32[128,128]{1,0:T(8,128)S(1)} custom-call(f32[128,128]{1,0:T(8,128)S(1)} %cholesky.275), custom_call_target="Cholesky" | custom-call | tf_op jit(solution)/shard_map/jit(cholesky)/cholesky | solution.py:72
  674.5 9.8 %custom-call.33 = f32[1,128,128]{1,2,0:T(8,128)S(1)} custom-call(f32[1,128,128]{2,1,0:T(8,128)S(1)} %get-tuple-element.46), custom_call_target="InvertDiagBlocksLowerTriangular" | custom-call | tf_op jit(solution)/shard_map/jit(cholesky)/cholesky | solution.py:72
  684.9 11.9 %cholesky.255 = f32[128,128]{1,0:T(8,128)S(1)} custom-call(f32[128,128]{1,0:T(8,128)S(1)} %convolution_subtract_fusion.2), custom_call_target="Cholesky" | custom-call | tf_op jit(solution)/shard_map/jit(cholesky)/cholesky | solution.py:72
  701.4 8.1 while.1
  709.6 39.3 %custom-call.34 = f32[4,128,128]{1,2,0:T(8,128)S(1)} custom-call(f32[4,128,128]{2,1,0:T(8,128)S(1)} %get-tuple-element.10), custom_call_target="InvertDiagBlocksLowerTriangular" | custom-call | tf_op jit(solution)/shard_map/jit(_solve_triangular)/triangular_solve | solution.py:73
  768.4 9.2 fusion
  782.4 12.3 %convolution_convert_fusion = bf16[2048,512]{1,0:T(8,128)(2,1)} fusion(bf16[3584,2048]{1,0:T(8,128)(2,1)} %get-tuple-element.31, f32[128,3584]{1,0:T(8,128)S(1)} %fusion.12, f32[128,3584]{1,0:T(8,128)S(1)} %fusion.13, f32[128,3584]{1,0:T(8,128)S(1)} %fusion.14, f32[128,3584]{1,0:T(8,128)S(1)} %fusion.15), kind=kOutput, calls=%fused_computation.23 | convolution fusion | flops 7531921408 | bytes 24117248 | tf_op jit(solution)/shard_map/dot_general | solution.py:76
  799.8 8.4 copy.9
  808.1 111.3 %all-gather.3.cloned.1.call-done = bf16[16384,512]{1,0:T(8,128)(2,1)} async-done(((bf16[2048,512]{1,0:T(8,128)(2,1)}), bf16[16384,512]{1,0:T(8,128)(2,1)}) %all-gather.3.cloned.1.call-update) | async-done | bytes 16777232 | tf_op jit(solution)/shard_map/all_gather | solution.py:77
  919.4 9.2 reduce_sum.21
  930.5 27.9 %multiply_subtract_fusion = f32[3584,2048]{1,0:T(8,128)} fusion(f32[3584,2048]{1,0:T(8,128)} %param.4, bf16[3584,2048]{1,0:T(8,128)(2,1)} %get-tuple-element.32, bf16[2048,512]{1,0:T(8,128)(2,1)} %copy-done.4, f32[128,3584]{1,0:T(8,128)} %copy-done.6, f32[128,3584]{1,0:T(8,128)} %copy-done.5, f32[128,3584]{1,0:T(8,128)} %copy-done.3, f32[128,3584]{1,0:T(8,128)} %copy-done.2), kind=kOutput, calls=%fused_computation.2 | convolution fusion | flops 7560232960 | bytes 82837504 | tf_op jit(solution)/shard_map/dot_general | solution.py:84
  958.3 11.7 %psum.7 = f32[512]{0:T(512)S(1)} all-reduce(f32[512]{0:T(512)S(1)} %fusion.6), channel_id=1, replica_groups=mesh['rows'=8,'cols'=4] {'cols'}, use_global_device_ids=true, to_apply=%region_10.11 | all-reduce | flops 512 | bytes 4096 | tf_op jit(solution)/shard_map/psum | solution.py:80
  (112 shorter events, 109.1 us)
Async XLA Ops:
  7.2 107.5 %copy-start = (bf16[2048,512]{1,0:T(8,128)(2,1)S(1)}, bf16[2048,512]{1,0:T(8,128)(2,1)}, u32[]{:S(2)}) copy-start(bf16[2048,512]{1,0:T(8,128)(2,1)} %param.5) | copy-start | bytes 6291460
  7.2 912.2 %all-gather.3.cloned.1.call-start = ((), (), s32[]{:S(2)}) async-start(), calls=%async_computation | async-start | bytes 18874368 | tf_op jit(solution)/shard_map/all_gather | solution.py:77
  29.5 85.1 %collective-permute-start.2 = (bf16[896,2048]{1,0:T(8,128)(2,1)}, bf16[896,2048]{1,0:T(8,128)(2,1)}, u32[]{:S(2)}, u32[]{:S(2)}) collective-permute-start(bf16[896,2048]{1,0:T(8,128)(2,1)} %get-tuple-element.29), channel_id=1, source_target_pairs={{0,3},{1,0},{2,1},{3,2},{4,7},{5,4},{6,5},{7,6},{8,11},{9,8},{10,9... | collective-permute-start | bytes 11010056 | tf_op jit(solution)/shard_map/ppermute | solution.py:12
  34.6 263.6 %collective-permute-start.1 = (bf16[896,2048]{1,0:T(8,128)(2,1)}, bf16[896,2048]{1,0:T(8,128)(2,1)}, u32[]{:S(2)}, u32[]{:S(2)}) collective-permute-start(bf16[896,2048]{1,0:T(8,128)(2,1)} %get-tuple-element.30), channel_id=1, source_target_pairs={{0,1},{1,2},{2,3},{3,0},{4,5},{5,6},{6,7},{7,4},{8,9},{9,10},{10,1... | collective-permute-start | bytes 11010056 | tf_op jit(solution)/shard_map/ppermute | solution.py:12
  34.6 335.6 %collective-permute-start = (bf16[896,2048]{1,0:T(8,128)(2,1)}, bf16[896,2048]{1,0:T(8,128)(2,1)}, u32[]{:S(2)}, u32[]{:S(2)}) collective-permute-start(bf16[896,2048]{1,0:T(8,128)(2,1)} %get-tuple-element.28), channel_id=1, source_target_pairs={{0,2},{1,3},{2,0},{3,1},{4,6},{5,7},{6,4},{7,5},{8,10},{9,11},{10,... | collective-permute-start | bytes 11010056 | tf_op jit(solution)/shard_map/ppermute | solution.py:12
  121.8 259.6 %collective-permute-start.5 = (bf16[896,512]{1,0:T(8,128)(2,1)}, bf16[896,512]{1,0:T(8,128)(2,1)S(1)}, u32[]{:S(2)}, u32[]{:S(2)}) collective-permute-start(bf16[896,512]{1,0:T(8,128)(2,1)} %convolution_convert_fusion.1), channel_id=1, source_target_pairs={{0,1},{1,2},{2,3},{3,0},{4,5},{5,6},{6,7},{7,4},{8,9},{9,10},{10,1... | collective-permute-start | bytes 2752520 | tf_op jit(solution)/shard_map/ppermute | solution.py:12
  305.4 76.1 %collective-permute-start.4 = (bf16[896,512]{1,0:T(8,128)(2,1)}, bf16[896,512]{1,0:T(8,128)(2,1)}, u32[]{:S(2)}, u32[]{:S(2)}) collective-permute-start(bf16[896,512]{1,0:T(8,128)(2,1)} %convolution_convert_fusion.2), channel_id=1, source_target_pairs={{0,3},{1,0},{2,1},{3,2},{4,7},{5,4},{6,5},{7,6},{8,11},{9,8},{10,9... | collective-permute-start | bytes 2752520 | tf_op jit(solution)/shard_map/ppermute | solution.py:12
  377.4 50.6 %collective-permute-start.3 = (bf16[896,512]{1,0:T(8,128)(2,1)}, bf16[896,512]{1,0:T(8,128)(2,1)}, u32[]{:S(2)}, u32[]{:S(2)}) collective-permute-start(bf16[896,512]{1,0:T(8,128)(2,1)} %convolution_convert_fusion.3), channel_id=1, source_target_pairs={{0,2},{1,3},{2,0},{3,1},{4,6},{5,7},{6,4},{7,5},{8,10},{9,11},{10,... | collective-permute-start | bytes 2752520 | tf_op jit(solution)/shard_map/ppermute | solution.py:12
  439.7 2.3 collective-permute-start.6
  443.1 0.8 copy-start.7
  443.9 8.4 collective-permute-start.7
  453.4 7.6 collective-permute-start.8
  461.2 6.7 collective-permute-start.9
  467.9 12.9 %collective-permute-start.10 = (f32[64,512]{0,1:T(8,128)S(1)}, f32[64,512]{0,1:T(8,128)S(1)}, u32[]{:S(2)}, u32[]{:S(2)}) collective-permute-start(f32[64,512]{0,1:T(8,128)S(1)} %add.223), channel_id=1, source_target_pairs={{0,2},{1,3},{2,0},{3,1},{4,6},{5,7},{6,4},{7,5},{8,10},{9,11},{10,... | collective-permute-start | bytes 393224 | tf_op jit(solution)/shard_map/ppermute | solution.py:16
  480.9 16.7 %collective-permute-start.11 = (f32[64,512]{0,1:T(8,128)S(1)}, f32[64,512]{0,1:T(8,128)S(1)}, u32[]{:S(2)}, u32[]{:S(2)}) collective-permute-start(f32[64,512]{0,1:T(8,128)S(1)} %add.224), channel_id=1, source_target_pairs={{0,16},{4,20},{8,24},{12,28},{16,0},{20,4},{24,8},{28,12},{1,17},{... | collective-permute-start | bytes 393224 | tf_op jit(solution)/shard_map/ppermute | solution.py:16
  492.8 44.8 %collective-permute-start.14 = (f32[896,512]{1,0:T(8,128)S(1)}, f32[896,512]{1,0:T(8,128)S(1)}, u32[]{:S(2)}, u32[]{:S(2)}) collective-permute-start(f32[896,512]{1,0:T(8,128)S(1)} %get-tuple-element.23), channel_id=1, source_target_pairs={{0,1},{1,2},{2,3},{3,0},{4,5},{5,6},{6,7},{7,4},{8,9},{9,10},{10,1... | collective-permute-start | bytes 5505032 | tf_op jit(solution)/shard_map/ppermute | solution.py:12
  494.6 119.5 %collective-permute-start.15 = (f32[896,512]{1,0:T(8,128)S(1)}, f32[896,512]{1,0:T(8,128)S(1)}, u32[]{:S(2)}, u32[]{:S(2)}) collective-permute-start(f32[896,512]{1,0:T(8,128)S(1)} %get-tuple-element.23), channel_id=1, source_target_pairs={{0,2},{1,3},{2,0},{3,1},{4,6},{5,7},{6,4},{7,5},{8,10},{9,11},{10,... | collective-permute-start | bytes 5505032 | tf_op jit(solution)/shard_map/ppermute | solution.py:12
  495.5 120.0 %collective-permute-start.16 = (f32[896,512]{1,0:T(8,128)S(1)}, f32[896,512]{1,0:T(8,128)S(1)}, u32[]{:S(2)}, u32[]{:S(2)}) collective-permute-start(f32[896,512]{1,0:T(8,128)S(1)} %get-tuple-element.23), channel_id=1, source_target_pairs={{0,3},{1,0},{2,1},{3,2},{4,7},{5,4},{6,5},{7,6},{8,11},{9,8},{10,9... | collective-permute-start | bytes 5505032 | tf_op jit(solution)/shard_map/ppermute | solution.py:12
  497.7 11.9 %collective-permute-start.12 = (f32[128,512]{0,1:T(8,128)S(1)}, f32[128,512]{0,1:T(8,128)S(1)}, u32[]{:S(2)}, u32[]{:S(2)}) collective-permute-start(f32[128,512]{0,1:T(8,128)S(1)} %pad_maximum_fusion.2), channel_id=1, source_target_pairs={{0,8},{4,12},{8,0},{12,4},{16,24},{20,28},{24,16},{28,20},{1,9},{5... | collective-permute-start | bytes 786440 | tf_op jit(solution)/shard_map/ppermute | solution.py:16
  509.8 107.0 %collective-permute-start.13 = (f32[256,512]{0,1:T(8,128)S(1)}, f32[256,512]{0,1:T(8,128)S(1)}, u32[]{:S(2)}, u32[]{:S(2)}) collective-permute-start(f32[256,512]{0,1:T(8,128)S(1)} %pad_maximum_fusion.1), channel_id=1, source_target_pairs={{0,4},{4,0},{8,12},{12,8},{16,20},{20,16},{24,28},{28,24},{1,5},{5... | collective-permute-start | bytes 1572872 | tf_op jit(solution)/shard_map/ppermute | solution.py:16
  752.1 42.6 %copy-start.2 = (f32[128,3584]{1,0:T(8,128)}, f32[128,3584]{1,0:T(8,128)S(1)}, u32[]{:S(2)}) copy-start(f32[128,3584]{1,0:T(8,128)S(1)} %fusion.15) | copy-start | bytes 5505028
  758.5 22.6 %copy-start.3 = (f32[128,3584]{1,0:T(8,128)}, f32[128,3584]{1,0:T(8,128)S(1)}, u32[]{:S(2)}) copy-start(f32[128,3584]{1,0:T(8,128)S(1)} %fusion.14) | copy-start | bytes 5505028
  768.4 12.7 %copy-start.5 = (f32[128,3584]{1,0:T(8,128)}, f32[128,3584]{1,0:T(8,128)S(1)}, u32[]{:S(2)}) copy-start(f32[128,3584]{1,0:T(8,128)S(1)} %fusion.13) | copy-start | bytes 5505028
  781.1 1.2 copy-start.6
  928.6 1.3 copy-start.4
  930.5 42.9 %copy-start.1 = (bf16[2048,512]{1,0:T(8,128)(2,1)S(1)}, bf16[2048,512]{1,0:T(8,128)(2,1)}, u32[]{:S(2)}) copy-start(bf16[2048,512]{1,0:T(8,128)(2,1)} %param.5) | copy-start | bytes 6291460
Sparse Core Ops, SparseCore 0:
  794.8 124.5 all-gather.2
